TPU v7x, 256 devices: a whole 4x4x8 slice. The times are simulated.
256 devices in a mesh: row: 8 (over y, core), col: 32 (over x, z).
Axes of the slice: x: 4, y: 4, z: 8, core: 2. Of those that a mesh axis runs over, the one named last changes fastest.
Arguments:
- tokens: bfloat16 [2048, 6144], P('row', 'col'), may hold values from -6 to 6
- cotangent: bfloat16 [2048, 6144], P('row', 'col'), may hold values from -6 to 6
- w_expand: bfloat16 [6144, 12288], P('row', 'col'), may hold values from -0.078125 to 0.078125
- w_reduce: bfloat16 [6144, 12288], P('row', 'col'), may hold values from -0.0546875 to 0.0546875
- expand_mean: bfloat16 [6144, 12288], P('row', 'col'), may hold values from -1 to 1
- expand_mean_scale: float32 [24, 12288], P('row', 'col'), may hold values from 4 to 16
- expand_var: bfloat16 [6144, 12288], P('row', 'col'), may hold values from 0.049804688 to 1
- expand_var_scale: float32 [24, 12288], P('row', 'col'), may hold values from 4 to 16
- reduce_mean: bfloat16 [6144, 12288], P('row', 'col'), may hold values from -1 to 1
- reduce_mean_scale: float32 [24, 12288], P('row', 'col'), may hold values from 4 to 16
- reduce_var: bfloat16 [6144, 12288], P('row', 'col'), may hold values from 0.049804688 to 1
- reduce_var_scale: float32 [24, 12288], P('row', 'col'), may hold values from 4 to 16
Outputs:
- grad_tokens: bfloat16 [2048, 6144], P('row', 'col')
- new_expand: bfloat16 [6144, 12288], P('row', 'col')
- expand_mean_next: bfloat16 [6144, 12288], P('row', 'col')
- expand_mean_scale_next: float32 [24, 12288], P('row', 'col')
- expand_var_next: bfloat16 [6144, 12288], P('row', 'col')
- expand_var_scale_next: float32 [24, 12288], P('row', 'col')
- new_reduce: bfloat16 [6144, 12288], P('row', 'col')
- reduce_mean_next: bfloat16 [6144, 12288], P('row', 'col')
- reduce_mean_scale_next: float32 [24, 12288], P('row', 'col')
- reduce_var_next: bfloat16 [6144, 12288], P('row', 'col')
- reduce_var_scale_next: float32 [24, 12288], P('row', 'col')
All inputs are finite; a program needn't handle non-finite values.
Results may differ from a plain program's by a relative error of at most 0.0049.
Values may be sent and summed in bfloat16 or wider, within the bound.
No kernel may reach another device: no remote copies, remote signals or barrier semaphores. Data moves between devices by JAX's collectives and lax.ppermute only.
A program may use at most 128 MiB of HBM per device.

v0:
```python
import jax
import jax.numpy as jnp
from jax import lax
from jax.sharding import PartitionSpec as P

STEP = 10
beta_one = 0.9
beta_two = 0.999
adam_eps = 1e-08
learn_rate = 0.001
decay_rate = 0.1
scale_eps = 1e-06


def gelu_pair(pre_act):
    cdf_part = 0.5 * (1.0 + lax.erf(pre_act * 0.7071067811865476))
    slope = cdf_part + pre_act * jnp.exp(-0.5 * pre_act * pre_act) * 0.3989422804014327
    return (pre_act * cdf_part, slope)


def spread_scale(values, scale):
    blocks = scale.shape[0]
    shaped = values.reshape(blocks, values.shape[0] // blocks, values.shape[1])
    return (shaped * scale[:, None, :]).reshape(values.shape)


def block_max(values, blocks):
    shaped = values.reshape(blocks, values.shape[0] // blocks, values.shape[1])
    return jnp.max(jnp.abs(shaped), axis=1) + scale_eps


def adam_step(weight, grad_w, mean_q, mean_scale, var_q, var_scale):
    blocks = mean_scale.shape[0]
    mean_new = (
        beta_one * spread_scale(mean_q.astype(jnp.float32), mean_scale) + (1.0 - beta_one) * grad_w
    )
    var_new = (
        beta_two * spread_scale(var_q.astype(jnp.float32), var_scale)
        + (1.0 - beta_two) * grad_w * grad_w
    )
    mean_hat = mean_new / (1.0 - beta_one**STEP)
    var_hat = var_new / (1.0 - beta_two**STEP)
    old_weight = weight.astype(jnp.float32)
    new_weight = (
        old_weight
        - learn_rate * (mean_hat / (jnp.sqrt(var_hat) + adam_eps) + decay_rate * old_weight)
    ).astype(jnp.bfloat16)
    mean_scale_next = block_max(mean_new, blocks)
    var_scale_next = block_max(var_new, blocks)
    mean_next = spread_scale(mean_new, 1.0 / mean_scale_next).astype(jnp.bfloat16)
    var_next = spread_scale(var_new, 1.0 / var_scale_next).astype(jnp.bfloat16)
    return (new_weight, mean_next, mean_scale_next, var_next, var_scale_next)


def contract_first(left, right):
    return lax.dot_general(
        left, right, (((0,), (0,)), ((), ())), preferred_element_type=jnp.float32
    )


def local(
    tokens,
    cotangent,
    w_expand,
    w_reduce,
    expand_mean,
    expand_mean_scale,
    expand_var,
    expand_var_scale,
    reduce_mean,
    reduce_mean_scale,
    reduce_var,
    reduce_var_scale,
):
    token_rows, cot_rows = (
        lax.all_gather(tokens, "col", axis=1, tiled=True),
        lax.all_gather(cotangent, "col", axis=1, tiled=True),
    )
    input_whole, cot_whole = (
        lax.all_to_all(token_rows, "row", split_axis=1, concat_axis=0, tiled=True),
        lax.all_to_all(cot_rows, "row", split_axis=1, concat_axis=0, tiled=True),
    )
    up_panel, down_panel = (
        lax.all_gather(w_expand, "row", axis=0, tiled=True),
        lax.all_gather(w_reduce, "row", axis=0, tiled=True),
    )
    pre_act = jnp.dot(token_rows, up_panel, preferred_element_type=jnp.float32)
    act_grad = jnp.dot(cot_rows, down_panel, preferred_element_type=jnp.float32)
    activated, slope = gelu_pair(pre_act)
    activated = activated.astype(jnp.bfloat16)
    pre_grad = (act_grad * slope).astype(jnp.bfloat16)
    grad_cols = lax.psum_scatter(
        lax.dot_general(
            up_panel, pre_grad, (((1,), (1,)), ((), ())), preferred_element_type=jnp.float32
        ),
        "col",
        scatter_dimension=0,
        tiled=True,
    )
    grad_tokens = grad_cols.T.astype(jnp.bfloat16)
    grad_expand = contract_first(input_whole, lax.all_gather(pre_grad, "row", axis=0, tiled=True))
    grad_reduce = contract_first(cot_whole, lax.all_gather(activated, "row", axis=0, tiled=True))
    first = adam_step(
        w_expand, grad_expand, expand_mean, expand_mean_scale, expand_var, expand_var_scale
    )
    second = adam_step(
        w_reduce, grad_reduce, reduce_mean, reduce_mean_scale, reduce_var, reduce_var_scale
    )
    return (
        grad_tokens,
        first[0],
        first[1],
        first[2],
        first[3],
        first[4],
        second[0],
        second[1],
        second[2],
        second[3],
        second[4],
    )


def solution(mesh):
    placed = (
        P("row", "col"),
        P("row", "col"),
        P("row", "col"),
        P("row", "col"),
        P("row", "col"),
        P("row", "col"),
        P("row", "col"),
        P("row", "col"),
        P("row", "col"),
        P("row", "col"),
        P("row", "col"),
        P("row", "col"),
    )
    return jax.shard_map(
        local,
        mesh=mesh,
        in_specs=placed,
        out_specs=(
            P("row", "col"),
            P("row", "col"),
            P("row", "col"),
            P("row", "col"),
            P("row", "col"),
            P("row", "col"),
            P("row", "col"),
            P("row", "col"),
            P("row", "col"),
            P("row", "col"),
            P("row", "col"),
        ),
        check_vma=False,
    )
```

profile of v0, /device:TPU:8, one launch (start us, length us, event | category | flops | bytes accessed | tf_op | source)
XLA Modules:
  0.0 555.6 jit_solution(1710327823756502407)
XLA Ops:
  10.0 82.9 %all-gather.11.cloned.1.call-done = bf16[256,6144]{0,1:T(8,128)(2,1)} async-done(((bf16[256,192]{0,1:T(8,128)(2,1)}), bf16[256,6144]{0,1:T(8,128)(2,1)}) %all-gather.11.cloned.1.call-update) | async-done | bytes 3145744 | tf_op jit(solution)/shard_map/all_gather | solution.py:76
  92.9 34.3 %all-gather.13.cloned.1.call-done = bf16[6144,384]{1,0:T(8,128)(2,1)} async-done(((bf16[768,384]{1,0:T(8,128)(2,1)}), bf16[6144,384]{1,0:T(8,128)(2,1)}) %all-gather.13.cloned.1.call-update) | async-done | bytes 4718608 | tf_op jit(solution)/shard_map/all_gather | solution.py:84
  127.2 5.8 %multiply_convert_fusion.4 = (bf16[256,384]{1,0:T(8,128)(2,1)}, f32[256,384]{1,0:T(8,128)S(1)}) fusion(bf16[256,6144]{0,1:T(8,128)(2,1)} %all-gather.11.cloned.1.call-done, bf16[6144,384]{1,0:T(8,128)(2,1)} %all-gather.13.cloned.1.call-done), kind=kOutput, calls=%fused_computation.30 | convolution fusion | flops 1208451072 | bytes 8454144 | tf_op jit(solution)/shard_map/dot_general | solution.py:87
  133.1 77.2 %all-gather.7.cloned.1.call-done = bf16[256,6144]{0,1:T(8,128)(2,1)} async-done(((bf16[256,192]{0,1:T(8,128)(2,1)}), bf16[256,6144]{0,1:T(8,128)(2,1)}) %all-gather.7.cloned.1.call-update) | async-done | bytes 3145744 | tf_op jit(solution)/shard_map/all_gather | solution.py:77
  210.2 34.2 %all-gather.9.cloned.1.call-done = bf16[6144,384]{1,0:T(8,128)(2,1)} async-done(((bf16[768,384]{1,0:T(8,128)(2,1)}), bf16[6144,384]{1,0:T(8,128)(2,1)}) %all-gather.9.cloned.1.call-update) | async-done | bytes 4718608 | tf_op jit(solution)/shard_map/all_gather | solution.py:85
  244.4 5.9 %fusion.8 = bf16[256,384]{1,0:T(8,128)(2,1)} fusion(bf16[256,6144]{0,1:T(8,128)(2,1)} %all-gather.7.cloned.1.call-done, bf16[6144,384]{1,0:T(8,128)(2,1)} %all-gather.9.cloned.1.call-done, f32[256,384]{1,0:T(8,128)S(1)} %get-tuple-element.82), kind=kOutput, calls=%fused_computation.24 | convolution fusion | flops 1208942592 | bytes 8454144 | tf_op jit(solution)/shard_map/dot_general | solution.py:88
  250.9 7.0 %convolution_bitcast_fusion = f32[6144,256]{0,1:T(8,128)} fusion(bf16[256,384]{1,0:T(8,128)(2,1)} %fusion.8, bf16[6144,384]{1,0:T(8,128)(2,1)} %all-gather.13.cloned.1.call-done), kind=kOutput, calls=%fused_computation | convolution fusion | flops 1207959552 | bytes 11206656 | tf_op jit(solution)/shard_map/dot_general | solution.py:93
  257.9 6.6 %copy.123 = f32[6144,256]{1,0:T(8,128)} copy(f32[6144,256]{0,1:T(8,128)} %convolution_bitcast_fusion) | data formatting | bytes 12582912
  266.4 49.7 %all_to_all.38 = bf16[256,8,768]{0,2,1:T(8,128)(2,1)} all-to-all(bf16[256,8,768]{0,2,1:T(8,128)(2,1)S(1)} %bitcast.38), channel_id=1, replica_groups=mesh['row'=8,'col'=32] {'row'}, dimensions={1} | all-to-all | bytes 6291456 | tf_op jit(solution)/shard_map/all_to_all | solution.py:80
  316.1 4.0 all-to-all-start.1
  320.2 2.1 copy.96
  325.5 2.7 copy.101
  329.3 2.7 copy.98
  332.0 2.1 copy.100
  337.4 2.7 copy.108
  341.2 2.7 copy.111
  343.8 2.1 copy.107
  346.0 2.1 copy.110
  348.1 4.7 copy.99
  352.8 4.3 all-to-all-done.1
  357.1 2.9 copy.109
  360.0 6.3 %fusion.18 = (f32[768,384]{0,1:T(8,128)}, f32[768,384]{0,1:T(8,128)S(1)}, f32[768,384]{0,1:T(8,128)S(1)}, f32[768,384]{0,1:T(8,128)S(1)}) fusion(f32[768,384]{0,1:T(8,128)} %copy.98, bf16[768,384]{0,1:T(8,128)(2,1)} %copy.97, f32[768,384]{0,1:T(8,128)} %copy.101, bf16[768,384]{0,1:T(8,128)(2,1)} %copy.100, ...), kind=kOutput, calls=%fused_computation.44 | convolution fusion | flops 1211793408 | bytes 12976128 | tf_op jit(solution)/shard_map/dot_general | solution.py:56
  366.3 2.7 copy.102
  377.8 2.7 copy.105
  380.5 3.5 multiply_convert_fusion.2
  384.0 2.3 copy.117
  388.4 2.1 copy.119
  390.5 6.4 %fusion.15 = (f32[768,384]{0,1:T(8,128)}, f32[768,384]{0,1:T(8,128)}, f32[768,384]{0,1:T(8,128)}, f32[768,384]{0,1:T(8,128)}) fusion(f32[768,384]{0,1:T(8,128)} %copy.108, bf16[768,384]{0,1:T(8,128)(2,1)} %copy.107, f32[768,384]{0,1:T(8,128)} %copy.111, bf16[768,384]{0,1:T(8,128)(2,1)} %copy.110, bf16[2048,384]{1,0:T(8,128)(2,1)} %all-gather.17.cloned.1.call-done, ...), kind=kOutput, calls=%fused_computation.42 | convolution fusion | flops 1211793408 | bytes 12976128 | tf_op jit(solution)/shard_map/dot_general | solution.py:56
  402.5 2.9 copy.115
  405.4 3.5 multiply_convert_fusion
  408.9 2.2 copy.120
  413.2 133.7 %reduce-scatter.4.cloned.1.call-done = f32[192,256]{1,0:T(8,128)} async-done(((f32[6144,256]{1,0:T(8,128)}), f32[192,256]{1,0:T(8,128)}) %reduce-scatter.4.cloned.1.call-update) | async-done | bytes 196624
  (66 shorter events, 34.4 us)
Async XLA Ops:
  7.2 85.7 %all-gather.11.cloned.1.call-start = ((), (), s32[]{:S(2)}) async-start(), calls=%async_computation.5 | async-start | bytes 3244032 | tf_op jit(solution)/shard_map/all_gather | solution.py:76
  7.9 119.3 %all-gather.13.cloned.1.call-start = ((), (), s32[]{:S(2)}) async-start(), calls=%async_computation.6 | async-start | bytes 5308416 | tf_op jit(solution)/shard_map/all_gather | solution.py:84
  8.7 201.6 %all-gather.7.cloned.1.call-start = ((), (), s32[]{:S(2)}) async-start(), calls=%async_computation.3 | async-start | bytes 3244032 | tf_op jit(solution)/shard_map/all_gather | solution.py:77
  9.4 235.0 %all-gather.9.cloned.1.call-start = ((), (), s32[]{:S(2)}) async-start(), calls=%async_computation.4 | async-start | bytes 5308416 | tf_op jit(solution)/shard_map/all_gather | solution.py:85
  10.0 350.0 %all-gather.15.cloned.1.call-start = ((), (), s32[]{:S(2)}) async-start(), calls=%async_computation.7 | async-start | bytes 1769472 | tf_op jit(solution)/shard_map/all_gather | solution.py:101
  250.3 140.2 %all-gather.17.cloned.1.call-start = ((), (), s32[]{:S(2)}) async-start(), calls=%async_computation.8 | async-start | bytes 1769472 | tf_op jit(solution)/shard_map/all_gather | solution.py:102
  250.9 296.1 %reduce-scatter.4.cloned.1.call-start = ((), (), s32[]{:S(2)}) async-start(), calls=%async_computation.9 | async-start | bytes 6488064
  264.5 1.9 copy-start
  316.1 41.0 %all-to-all-start.1 = ((bf16[256,8,768]{0,2,1:T(8,128)(2,1)}), bf16[256,8,768]{0,2,1:T(8,128)(2,1)S(1)}, u32[]{:S(2)}, u32[]{:S(2)}) async-start(bf16[256,8,768]{0,2,1:T(8,128)(2,1)} %bitcast.39), calls=%async_computation.1 | async-start | bytes 6291456 | tf_op jit(solution)/shard_map/all_to_all | solution.py:81
  320.2 4.3 copy-start.8
  325.5 2.7 copy-start.9
  332.0 4.3 copy-start.10
  337.4 2.7 copy-start.11
  370.4 1.6 copy-start.5
  384.0 6.5 %copy-start.1 = (bf16[8,256,768]{2,1,0:T(8,128)(2,1)S(1)}, bf16[8,256,768]{2,1,0:T(8,128)(2,1)}, u32[]{:S(2)}) copy-start(bf16[8,256,768]{2,1,0:T(8,128)(2,1)} %copy.109) | copy-start | bytes 9437188
  398.5 1.3 copy-start.4
  402.5 2.9 copy-start.2
  402.5 2.9 copy-start.3
  408.9 2.2 copy-start.7
  408.9 3.3 copy-start.6
Sparse Core Ops, SparseCore 0:
  10.6 82.2 all-gather.10
  94.7 32.4 all-gather.12
  129.8 80.3 all-gather.6
  211.9 32.4 all-gather.8
  250.4 27.9 all-gather.14
  280.1 34.5 all-gather.16
  318.7 228.2 reduce-scatter.3
where the time goes:
time: 557 us; the launch traced here: 556 us
  waiting for transfers between devices  370 us (66%)
  local copies, waits for them, and re-layouts  75.1 us (13%)
  blocking collectives  49.7 us (9%)
  matrix products  31.3 us (6%)
  between operations  14.2 us (3%)
  other arithmetic  11.2 us (2%)
    unnamed x8, waiting for transfers between devices  137 us
    all_gather x1, waiting for transfers between devices, local(): lax.all_gather(tokens, 'col', axis=1, tiled=True)  82.9 us
    all_gather x1, waiting for transfers between devices, local(): lax.all_gather(cotangent, 'col', axis=1, tiled=True)  77.2 us
    all_to_all x1, blocking collectives, local(): lax.all_to_all(token_rows, 'row', split_axis=1, concat_axis=0, tiled=True)  49.7 us
    unnamed x39, local copies, waits for them, and re-layouts  35.3 us
    all_gather x1, waiting for transfers between devices, local(): lax.all_gather(w_expand, 'row', axis=0, tiled=True)  34.3 us
    all_gather x1, waiting for transfers between devices, local(): lax.all_gather(w_reduce, 'row', axis=0, tiled=True)  34.2 us
    mul x16, local copies, waits for them, and re-layouts, spread_scale(): return (shaped * scale[:, None, :]).reshape(values.shape)  26.2 us
  transfers between devices with their start and end apart: 8, of which 6 were waited for; matrix products, arithmetic and copies ran while one was open for 19% of the time, Pallas kernels for 0%

commit v1 on v0

--- a/solution.py
+++ b/solution.py
@@ -72,9 +72,21 @@
     reduce_var,
     reduce_var_scale,
 ):
+
+    def meshes_map(row_data, mesh_dim):
+        return jnp.concatenate(
+            lax.all_to_all(
+                jnp.stack(lax.axis_size(mesh_dim) * [row_data], axis=0),
+                axis_name=mesh_dim,
+                split_axis=0,
+                concat_axis=0,
+            ),
+            axis=1,
+        )
+
     token_rows, cot_rows = (
         lax.all_gather(tokens, "col", axis=1, tiled=True),
-        lax.all_gather(cotangent, "col", axis=1, tiled=True),
+        meshes_map(cotangent, "col"),
     )
     input_whole, cot_whole = (
         lax.all_to_all(token_rows, "row", split_axis=1, concat_axis=0, tiled=True),

time: 557 us -> 503 us (0.903)
  waiting for transfers between devices: 370 us -> 302 us
  starting transfers between devices: 4.3 us -> 15.7 us
    all_gather x1 -> x0, waiting for transfers between devices: 77.2 us -> none  [local(): lax.all_gather(cotangent, 'col', axis=1, tiled=True)]
    all_to_all x0 -> x1, starting transfers between devices: none -> 11.4 us  [meshes_map(): lax.all_to_all(jnp.stack(lax.axis_size(mesh_dim) * [row_data], axis=0), a...]
    all_gather x1, waiting for transfers between devices: 82.9 us -> 92.6 us  [local(): lax.all_gather(tokens, 'col', axis=1, tiled=True)]
    unnamed x8 -> x7, waiting for transfers between devices: 137 us -> 136 us
    unnamed x39 -> x41, local copies, waits for them, and re-layouts: 35.3 us -> 35.3 us
  transfers between devices with their start and end apart: 8 -> 8, of which waited for: 6 -> 5; matrix products, arithmetic and copies ran while one was open for 19% -> 22% of each run, Pallas kernels for 0% -> 0%
where the time goes in v1:
time: 503 us; the launch traced here: 502 us
  waiting for transfers between devices  302 us (60%)
  local copies, waits for them, and re-layouts  77.1 us (15%)
  blocking collectives  49.7 us (10%)
  matrix products  31.3 us (6%)
  starting transfers between devices  15.7 us (3%)
  between operations  14.2 us (3%)
  other arithmetic  11.2 us (2%)
    unnamed x7, waiting for transfers between devices  136 us
    all_gather x1, waiting for transfers between devices, local(): lax.all_gather(tokens, 'col', axis=1, tiled=True)  92.6 us
    all_to_all x1, blocking collectives, local(): lax.all_to_all(token_rows, 'row', split_axis=1, concat_axis=0, tiled=True)  49.7 us
    all_gather x1, waiting for transfers between devices, local(): lax.all_gather(w_expand, 'row', axis=0, tiled=True)  36.6 us
    unnamed x41, local copies, waits for them, and re-layouts  35.3 us
    all_gather x1, waiting for transfers between devices, local(): lax.all_gather(w_reduce, 'row', axis=0, tiled=True)  32.8 us
    mul x16, local copies, waits for them, and re-layouts, spread_scale(): return (shaped * scale[:, None, :]).reshape(values.shape)  26.2 us
    dot_general x2, matrix products, contract_first(): lax.dot_general(left, right, (((0,), (0,)), ((), ())), preferred_element_...  12.6 us
  transfers between devices with their start and end apart: 8, of which 5 were waited for; matrix products, arithmetic and copies ran while one was open for 22% of the time, Pallas kernels for 0%

profile of v1, /device:TPU:8, one launch (start us, length us, event | category | flops | bytes accessed | tf_op | source)
XLA Modules:
  0.0 501.6 jit_solution(6521275776533425224)
XLA Ops:
  11.4 11.4 %all-to-all-start = ((bf16[32,256,192]{1,2,0:T(8,128)(2,1)}), bf16[32,256,192]{1,2,0:T(8,128)(2,1)}, u32[]{:S(2)}, u32[]{:S(2)}) async-start(bf16[32,256,192]{1,2,0:T(8,128)(2,1)} %stack.2), calls=%async_computation | async-start | bytes 6291456 | tf_op jit(solution)/shard_map/all_to_all | solution.py:78
  22.9 92.6 %all-gather.8.cloned.1.call-done = bf16[256,6144]{0,1:T(8,128)(2,1)} async-done(((bf16[256,192]{0,1:T(8,128)(2,1)}), bf16[256,6144]{0,1:T(8,128)(2,1)}) %all-gather.8.cloned.1.call-update) | async-done | bytes 3145744 | tf_op jit(solution)/shard_map/all_gather | solution.py:88
  115.6 36.6 %all-gather.10.cloned.1.call-done = bf16[6144,384]{1,0:T(8,128)(2,1)} async-done(((bf16[768,384]{1,0:T(8,128)(2,1)}), bf16[6144,384]{1,0:T(8,128)(2,1)}) %all-gather.10.cloned.1.call-update) | async-done | bytes 4718608 | tf_op jit(solution)/shard_map/all_gather | solution.py:96
  152.1 5.8 %multiply_convert_fusion.4 = (bf16[256,384]{1,0:T(8,128)(2,1)}, f32[256,384]{1,0:T(8,128)S(1)}) fusion(bf16[256,6144]{0,1:T(8,128)(2,1)} %all-gather.8.cloned.1.call-done, bf16[6144,384]{1,0:T(8,128)(2,1)} %all-gather.10.cloned.1.call-done), kind=kOutput, calls=%fused_computation.30 | convolution fusion | flops 1208451072 | bytes 8454144 | tf_op jit(solution)/shard_map/dot_general | solution.py:99
  158.0 32.8 %all-gather.6.cloned.1.call-done = bf16[6144,384]{1,0:T(8,128)(2,1)} async-done(((bf16[768,384]{1,0:T(8,128)(2,1)}), bf16[6144,384]{1,0:T(8,128)(2,1)}) %all-gather.6.cloned.1.call-update) | async-done | bytes 4718608 | tf_op jit(solution)/shard_map/all_gather | solution.py:97
  190.8 5.9 %fusion.8 = bf16[256,384]{1,0:T(8,128)(2,1)} fusion(bf16[256,6144]{0,1:T(8,128)(2,1)} %bitcast.1, bf16[6144,384]{1,0:T(8,128)(2,1)} %all-gather.6.cloned.1.call-done, f32[256,384]{1,0:T(8,128)S(1)} %get-tuple-element.82), kind=kOutput, calls=%fused_computation.24 | convolution fusion | flops 1208942592 | bytes 8454144 | tf_op jit(solution)/shard_map/dot_general | solution.py:100
  197.3 7.0 %convolution_bitcast_fusion = f32[6144,256]{0,1:T(8,128)} fusion(bf16[256,384]{1,0:T(8,128)(2,1)} %fusion.8, bf16[6144,384]{1,0:T(8,128)(2,1)} %all-gather.10.cloned.1.call-done), kind=kOutput, calls=%fused_computation | convolution fusion | flops 1207959552 | bytes 11206656 | tf_op jit(solution)/shard_map/dot_general | solution.py:105
  204.3 6.6 %copy.125 = f32[6144,256]{1,0:T(8,128)} copy(f32[6144,256]{0,1:T(8,128)} %convolution_bitcast_fusion) | data formatting | bytes 12582912
  212.8 49.7 %all_to_all.43 = bf16[256,8,768]{0,2,1:T(8,128)(2,1)} all-to-all(bf16[256,8,768]{0,2,1:T(8,128)(2,1)S(1)} %bitcast.42), channel_id=1, replica_groups=mesh['row'=8,'col'=32] {'row'}, dimensions={1} | all-to-all | bytes 6291456 | tf_op jit(solution)/shard_map/all_to_all | solution.py:92
  262.5 4.0 all-to-all-start.2
  266.6 2.1 copy.98
  271.9 2.7 copy.100
  275.7 2.7 copy.103
  278.4 2.1 copy.102
  283.8 2.7 copy.110
  287.6 2.7 copy.113
  290.2 2.1 copy.109
  292.4 2.1 copy.112
  294.5 4.7 copy.101
  299.2 4.3 all-to-all-done.2
  303.5 2.9 copy.111
  306.4 6.3 %fusion.18 = (f32[768,384]{0,1:T(8,128)}, f32[768,384]{0,1:T(8,128)S(1)}, f32[768,384]{0,1:T(8,128)S(1)}, f32[768,384]{0,1:T(8,128)S(1)}) fusion(f32[768,384]{0,1:T(8,128)} %copy.100, bf16[768,384]{0,1:T(8,128)(2,1)} %copy.99, f32[768,384]{0,1:T(8,128)} %copy.103, bf16[768,384]{0,1:T(8,128)(2,1)} %copy.102, ...), kind=kOutput, calls=%fused_computation.44 | convolution fusion | flops 1211793408 | bytes 12976128 | tf_op jit(solution)/shard_map/dot_general | solution.py:56
  312.7 2.7 copy.104
  324.2 2.7 copy.107
  326.9 3.5 multiply_convert_fusion.2
  330.4 2.3 copy.119
  334.8 2.1 copy.121
  336.9 6.4 %fusion.15 = (f32[768,384]{0,1:T(8,128)}, f32[768,384]{0,1:T(8,128)}, f32[768,384]{0,1:T(8,128)}, f32[768,384]{0,1:T(8,128)}) fusion(f32[768,384]{0,1:T(8,128)} %copy.110, bf16[768,384]{0,1:T(8,128)(2,1)} %copy.109, f32[768,384]{0,1:T(8,128)} %copy.113, bf16[768,384]{0,1:T(8,128)(2,1)} %copy.112, bf16[2048,384]{1,0:T(8,128)(2,1)} %all-gather.14.cloned.1.call-done, ...), kind=kOutput, calls=%fused_computation.42 | convolution fusion | flops 1211793408 | bytes 12976128 | tf_op jit(solution)/shard_map/dot_general | solution.py:56
  348.9 2.9 copy.117
  351.8 3.5 multiply_convert_fusion
  355.3 2.2 copy.122
  359.6 133.4 %reduce-scatter.4.cloned.1.call-done = f32[192,256]{1,0:T(8,128)} async-done(((f32[6144,256]{1,0:T(8,128)}), f32[192,256]{1,0:T(8,128)}) %reduce-scatter.4.cloned.1.call-update) | async-done | bytes 196624
  (68 shorter events, 35.8 us)
Async XLA Ops:
  7.2 2.2 copy-start.8
  7.2 108.4 %all-gather.8.cloned.1.call-start = ((), (), s32[]{:S(2)}) async-start(), calls=%async_computation.5 | async-start | bytes 3244032 | tf_op jit(solution)/shard_map/all_gather | solution.py:88
  7.9 144.2 %all-gather.10.cloned.1.call-start = ((), (), s32[]{:S(2)}) async-start(), calls=%async_computation.6 | async-start | bytes 5308416 | tf_op jit(solution)/shard_map/all_gather | solution.py:96
  8.7 182.2 %all-gather.6.cloned.1.call-start = ((), (), s32[]{:S(2)}) async-start(), calls=%async_computation.4 | async-start | bytes 5308416 | tf_op jit(solution)/shard_map/all_gather | solution.py:97
  11.4 146.6 %all-to-all-start = ((bf16[32,256,192]{1,2,0:T(8,128)(2,1)}), bf16[32,256,192]{1,2,0:T(8,128)(2,1)}, u32[]{:S(2)}, u32[]{:S(2)}) async-start(bf16[32,256,192]{1,2,0:T(8,128)(2,1)} %stack.2), calls=%async_computation | async-start | bytes 6291456 | tf_op jit(solution)/shard_map/all_to_all | solution.py:78
  22.9 283.5 %all-gather.12.cloned.1.call-start = ((), (), s32[]{:S(2)}) async-start(), calls=%async_computation.7 | async-start | bytes 1769472 | tf_op jit(solution)/shard_map/all_gather | solution.py:113
  196.7 140.2 %all-gather.14.cloned.1.call-start = ((), (), s32[]{:S(2)}) async-start(), calls=%async_computation.8 | async-start | bytes 1769472 | tf_op jit(solution)/shard_map/all_gather | solution.py:114
  197.3 295.7 %reduce-scatter.4.cloned.1.call-start = ((), (), s32[]{:S(2)}) async-start(), calls=%async_computation.9 | async-start | bytes 6488064
  210.9 1.9 copy-start
  262.5 41.0 %all-to-all-start.2 = ((bf16[256,8,768]{0,2,1:T(8,128)(2,1)}), bf16[256,8,768]{0,2,1:T(8,128)(2,1)S(1)}, u32[]{:S(2)}, u32[]{:S(2)}) async-start(bf16[256,8,768]{0,2,1:T(8,128)(2,1)} %bitcast.15), calls=%async_computation.2 | async-start | bytes 6291456 | tf_op jit(solution)/shard_map/all_to_all | solution.py:93
  266.6 4.3 copy-start.9
  271.9 2.7 copy-start.10
  278.4 4.3 copy-start.11
  283.8 2.7 copy-start.12
  316.7 1.6 copy-start.5
  330.4 6.5 %copy-start.1 = (bf16[8,256,768]{2,1,0:T(8,128)(2,1)S(1)}, bf16[8,256,768]{2,1,0:T(8,128)(2,1)}, u32[]{:S(2)}) copy-start(bf16[8,256,768]{2,1,0:T(8,128)(2,1)} %copy.111) | copy-start | bytes 9437188
  344.9 1.3 copy-start.4
  348.9 2.9 copy-start.2
  348.9 2.9 copy-start.3
  355.3 2.2 copy-start.7
  355.3 3.3 copy-start.6
Sparse Core Ops, SparseCore 0:
  10.6 104.9 all-gather.7
  117.4 34.7 all-gather.9
  154.0 36.8 all-gather.5
  196.8 27.9 all-gather.11
  226.5 34.5 all-gather.13
  264.9 228.0 reduce-scatter.3
